TPU v7x, 32 devices: a whole 2x2x4 slice. The times are simulated.
32 devices in a mesh: dp: 8 (over z, x), rep: 4 (over y, core).
Axes of the slice: x: 2, y: 2, z: 4, core: 2. Of those that a mesh axis runs over, the one named last changes fastest.
Arguments:
- grad: bfloat16 [8, 512, 512], P(None, 'dp'), may hold values from -6 to 6
- block_slot: int32 [8], replicated, may hold values from 0 to 15, as said below
- left_stat: float32 [16, 512, 512], P('dp', 'rep'), may hold values from -6 to 6
- right_stat: float32 [16, 512, 512], P('dp', 'rep'), may hold values from -6 to 6
- left_root: bfloat16 [16, 512, 512], P('dp')
- right_root: bfloat16 [16, 512, 512], P('dp')
- graft_acc: float32 [16, 512, 512], P('dp'), may hold values from 0.25 to 4
Outputs:
- update: bfloat16 [8, 512, 512], P(None, 'dp', 'rep')
- new_left: float32 [16, 512, 512], P('dp', 'rep')
- new_right: float32 [16, 512, 512], P('dp', 'rep')
- new_graft: float32 [16, 512, 512], P('dp')
Inputs may be any that keep to these rules, and one draw needn't show every extreme that they name: `block_slot`: distinct slot numbers; slot s belongs to owner s // 2, an index of dp, so an owner holds at most 2 blocks, and some owner holds exactly 2.
All inputs are finite; a program needn't handle non-finite values.
Results may differ from a plain program's by a relative error of at most 0.0049.
Values may be sent and summed in bfloat16 or wider, within the bound.
A program may use at most 64 MiB of HBM per device.

v0:
```python
import functools

import jax
import jax.numpy as jnp
from jax import lax
from jax.experimental import pallas as pl
from jax.experimental.pallas import tpu as pltpu
from jax.sharding import PartitionSpec as P

decay_rate = 0.99
epsilon = 1e-06


def local_plain(grad, block_slot, left_stat, right_stat, left_root, right_root, graft_acc):
    owners = lax.axis_size("dp")
    replicas = lax.axis_size("rep")
    blocks, band_rows, block_size = grad.shape
    capacity = left_stat.shape[0]
    slab_cols = block_size // replicas
    column = lax.axis_index("rep") * slab_cols
    own_cols = lax.dynamic_slice_in_dim(grad, column, slab_cols, 2)
    targets = jnp.arange(owners * capacity, dtype=jnp.int32)
    placing = (targets[:, None] == block_slot[None, :]).astype(jnp.bfloat16)
    packed = jnp.dot(
        placing, own_cols.reshape(blocks, band_rows * slab_cols), preferred_element_type=jnp.float32
    ).astype(jnp.bfloat16)
    packed = packed.reshape(owners, capacity, band_rows, slab_cols)
    arrived = lax.all_to_all(packed, "dp", split_axis=0, concat_axis=2, tiled=True)[0]
    gathered = lax.all_gather(arrived, "rep", axis=2, tiled=True)
    row_part = lax.dynamic_slice_in_dim(gathered, column, slab_cols, 1)
    left_term = jnp.einsum("sik,sjk->sij", row_part, gathered, preferred_element_type=jnp.float32)
    right_term = jnp.einsum("ski,skj->sij", arrived, gathered, preferred_element_type=jnp.float32)
    left_new = decay_rate * left_stat + (1.0 - decay_rate) * left_term
    right_new = decay_rate * right_stat + (1.0 - decay_rate) * right_term
    widened = gathered.astype(jnp.float32)
    graft_new = decay_rate * graft_acc + (1.0 - decay_rate) * widened * widened
    direction = widened / (jnp.sqrt(graft_new) + epsilon)
    graft_norm = jnp.sqrt(jnp.sum(direction * direction, axis=(1, 2)))
    middle = jnp.einsum(
        "sik,skj->sij", gathered, right_root, preferred_element_type=jnp.float32
    ).astype(jnp.bfloat16)
    full_precond = jnp.einsum("sik,skj->sij", left_root, middle, preferred_element_type=jnp.float32)
    squares = jnp.sum(full_precond * full_precond, axis=(1, 2))
    precond = lax.dynamic_slice_in_dim(full_precond, column, slab_cols, 2)
    graft_scale = graft_norm / (jnp.sqrt(squares) + epsilon)
    out_slab = (graft_scale[:, None, None] * precond).astype(jnp.bfloat16)
    returned = lax.all_to_all(out_slab[None], "dp", split_axis=2, concat_axis=0, tiled=True)
    spread = jnp.dot(
        placing.T,
        returned.reshape(owners * capacity, band_rows * slab_cols),
        preferred_element_type=jnp.float32,
    ).astype(jnp.bfloat16)
    update = spread.reshape(blocks, band_rows, slab_cols)
    return (update, left_new, right_new, graft_new)

def flipped(index, mask):
    bit = 1
    result = index
    while bit <= mask:
        if mask & bit:
            result = result + bit * (1 - 2 * ((index // bit) % 2))
        bit *= 2
    return result


def kernel(
    owners, replicas, slot_ref, grad_hbm, left_hbm, right_hbm, lroot_hbm, rroot_hbm, graft_hbm,
    update_ref, left, right, graft,
    own_grad, pack, placed, lroot, rroot, middle, precond, slab, returned,
    load_sem, own_sem, send1, recv1, send_y, recv_y, send_c, recv_c, send3, recv3,
):
    me = lax.axis_index("dp")
    rep = lax.axis_index("rep")
    blocks, band, size = own_grad.shape
    capacity = placed.shape[0]
    slab_cols = slab.shape[2]
    peers = replicas // 2
    partner = flipped(rep, 1)

    def peer(j):
        return (rep + 2 * j) % replicas

    def cols_of(index):
        return pl.ds(pl.multiple_of(index * slab_cols, slab_cols), slab_cols)

    def rows_of(owner):
        return pl.ds(pl.multiple_of(owner * band, band), band)

    def remote(src, dst, ssem, rsem, device):
        return pltpu.make_async_remote_copy(
            src_ref=src, dst_ref=dst, send_sem=ssem, recv_sem=rsem,
            device_id=device, device_id_type=pl.DeviceIdType.MESH,
        )

    cols = cols_of(rep)
    barrier = pltpu.get_barrier_semaphore()
    others = [(flipped(me, k), rep) for k in range(1, owners)]
    others += [(me, partner)] + [(me, peer(j)) for j in range(1, peers)]
    for device in others:
        pl.semaphore_signal(barrier, inc=1, device_id=device, device_id_type=pl.DeviceIdType.MESH)

    grad_load = pltpu.make_async_copy(grad_hbm, own_grad, load_sem.at[0])
    grad_load.start()
    loads = []
    for n, (src, dst) in enumerate(
        ((graft_hbm, graft), (rroot_hbm, rroot), (lroot_hbm, lroot), (left_hbm, left), (right_hbm, right))
    ):
        loads.append(pltpu.make_async_copy(src, dst, load_sem.at[n + 1]))
        loads[n].start()

    grad_load.wait()
    def find(slot):
        block = jnp.int32(0)
        named = jnp.int32(0)
        for b in range(blocks):
            hit = slot_ref[b] == slot
            block = jnp.where(hit, b, block)
            named = jnp.where(hit, 1, named)
        return block, named > 0

    for s in range(owners * capacity):
        block, named = find(s)
        for j in range(peers):
            tile = own_grad[block, :, cols_of(peer(j))]
            pack[j, s // capacity, s % capacity] = jnp.where(named, tile, jnp.zeros_like(tile))
    for c in range(capacity):
        block, named = find(me * capacity + c)
        tile = own_grad[block]
        placed[c, rows_of(me), :] = jnp.where(named, tile, jnp.zeros_like(tile))

    pl.semaphore_wait(barrier, len(others))

    half = owners // 2
    far = sorted(range(half, owners), key=lambda k: (k % 2, k))
    near = list(range(1, half))
    outward = []
    firsts = {}
    for c in range(capacity):
        for k in far + near:
            to = flipped(me, k)
            for j in range(peers if k < half else 1):
                copy = remote(
                    pack.at[j, to, c], placed.at[c, rows_of(me), cols_of(peer(j))],
                    send1.at[j, c, k], recv1.at[j, c, k], (to, rep),
                )
                copy.start()
                firsts[j, c, k] = copy
                outward.append(copy)

    norms = [jnp.zeros((band // 4, size), jnp.float32) for _ in range(capacity)]
    squares = [jnp.zeros((1, 1), jnp.float32) for _ in range(capacity)]
    thirds = {}
    tasks = []

    def multiply(c, q):
        part = pl.ds(q * size, size)
        full = jnp.dot(lroot[c, part, :], middle[c], preferred_element_type=jnp.float32)
        precond[c, part, :] = full
        squares[c] = squares[c] + jnp.sum(full * full, axis=(0, 1), keepdims=True)

    def finish(c):
        graft_norm = jnp.sqrt(jnp.sum(norms[c], axis=(0, 1), keepdims=True))
        scale = graft_norm / (jnp.sqrt(squares[c]) + epsilon)
        slab[c] = (scale * precond[c, :, cols]).astype(jnp.bfloat16)
        mine = returned.at[me * capacity + c]
        for k in far + near:
            to = flipped(me, k)
            thirds[c, k] = remote(slab.at[c, rows_of(to), :], mine, send3.at[c, k], recv3.at[c, k], (to, rep))
            thirds[c, k].start()
            outward.append(thirds[c, k])
        thirds[c, 0] = pltpu.make_async_copy(slab.at[c, rows_of(me), :], mine, own_sem.at[c])
        thirds[c, 0].start()

    along_y = {}
    across = {}
    def forward(c, k):
        for j in range(peers if k < half else 1):
            firsts[j, c, k].wait_recv()
        rows = rows_of(flipped(me, k))
        if k >= half:
            piece = placed.at[c, rows, cols]
            for j in range(1, peers):
                copy = remote(piece, piece, send_y.at[j, c, k], recv_y.at[j, c, k], (me, peer(j)))
                copy.start()
                along_y[j, c, k] = copy
        for j in range(peers if k < half else 1):
            piece = placed.at[c, rows, cols_of(peer(j))]
            copy = remote(piece, piece, send_c.at[j, c, k], recv_c.at[j, c, k], (me, partner))
            copy.start()
            across[j, c, k] = copy

    def relay(c, k):
        for j in range(1, peers):
            along_y[j, c, k].wait_recv()
            theirs = (rep + replicas - 2 * j) % replicas
            piece = placed.at[c, rows_of(flipped(me, k)), cols_of(theirs)]
            copy = remote(piece, piece, send_c.at[j, c, k], recv_c.at[j, c, k], (me, partner))
            copy.start()
            across[j, c, k] = copy

    def absorb(c, k):
        if k > 0:
            for j in range(peers):
                across[j, c, k].wait_recv()
        rows = rows_of(flipped(me, k))
        middle[c, rows, :] = jnp.dot(
            placed[c, rows, :], rroot[c], preferred_element_type=jnp.float32
        ).astype(jnp.bfloat16)
        for g in range(4):
            part = pl.ds(pl.multiple_of(flipped(me, k) * band + g * (band // 4), band // 4), band // 4)
            wide = placed[c, part, :].astype(jnp.float32)
            fresh = decay_rate * graft[c, part, :] + (1.0 - decay_rate) * wide * wide
            graft[c, part, :] = fresh
            direction = wide / (jnp.sqrt(fresh) + epsilon)
            norms[c] = norms[c] + direction * direction
        left_over[c] -= 1
        if left_over[c] == 0:
            tasks.extend(functools.partial(multiply, c, q) for q in range(1))
            tasks.append(functools.partial(finish, c))

    left_over = [owners] * capacity
    arrivals = near[:1] + far[:1] + near[1:2] + far[1:2] + near[2:] + far[2:]
    lag_y = 8
    lag_c = 5
    events = []
    for n, (c, k) in enumerate((c, k) for c in range(capacity) for k in arrivals):
        events.append((n, 0, forward, c, k))
        if k >= half:
            events.append((n + lag_y, 1, relay, c, k))
        events.append((n + lag_c + (lag_y if k >= half else 0), 2, absorb, c, k))
    events.sort(key=lambda event: event[:2])
    begun = 0
    for event in events:
        if event[2] is absorb and not begun:
            begun = 1
            for load in loads[:3]:
                load.wait()
            for c in range(capacity):
                absorb(c, 0)
        if tasks:
            tasks.pop(0)()
        event[2](*event[3:])
    for task in tasks:
        task()

    loads[3].wait()
    loads[4].wait()
    for c in range(capacity):
        term = lax.dot_general(
            placed[c, cols, :], placed[c], (((1,), (1,)), ((), ())), preferred_element_type=jnp.float32
        )
        left[c] = decay_rate * left[c] + (1.0 - decay_rate) * term
        term = lax.dot_general(
            placed[c, :, cols], placed[c], (((0,), (0,)), ((), ())), preferred_element_type=jnp.float32
        )
        right[c] = decay_rate * right[c] + (1.0 - decay_rate) * term

    for copy in list(along_y.values()) + list(across.values()):
        copy.wait_send()
    for (c, k), copy in thirds.items():
        if k == 0:
            copy.wait()
        else:
            copy.wait_recv()
    for b in range(blocks):
        update_ref[b] = returned[slot_ref[b]]
    for copy in outward:
        copy.wait_send()


def write_out(*refs):
    n = (len(refs) - 1) // 2
    sem = refs[-1]
    copies = [pltpu.make_async_copy(refs[i], refs[n + i], sem.at[i]) for i in range(n)]
    for copy in copies:
        copy.start()
    for copy in copies:
        copy.wait()


def local(grad, block_slot, left_stat, right_stat, left_root, right_root, graft_acc):
    owners = lax.axis_size("dp")
    replicas = lax.axis_size("rep")
    blocks, band, size = grad.shape
    capacity = left_stat.shape[0]
    slab_cols = size // replicas
    power_of_two = owners & (owners - 1) == 0 and owners >= 4
    if slab_cols % 128 or band % 64 or replicas % 2 or not power_of_two:
        return local_plain(grad, block_slot, left_stat, right_stat, left_root, right_root, graft_acc)
    peers = replicas // 2
    slots = owners * capacity
    f32, bf16 = jnp.float32, jnp.bfloat16
    vmem = pltpu.VMEM
    dma = pltpu.SemaphoreType.DMA
    anywhere = pl.BlockSpec(memory_space=pltpu.HBM)
    inside = pl.BlockSpec(memory_space=vmem)
    results = (
        ((blocks, band, slab_cols), bf16),
        (left_stat.shape, f32),
        (right_stat.shape, f32),
        (graft_acc.shape, f32),
    )
    held = pl.pallas_call(
        functools.partial(kernel, owners, replicas),
        out_shape=tuple(vmem(*r) for r in results),
        in_specs=[pl.BlockSpec(memory_space=pltpu.SMEM)] + [anywhere] * 6,
        out_specs=(inside,) * 4,
        scratch_shapes=[
            vmem((blocks, band, size), bf16),
            vmem((peers, owners, capacity, band, slab_cols), bf16),
            vmem((capacity, size, size), bf16),
            vmem(left_root.shape, bf16),
            vmem(right_root.shape, bf16),
            vmem((capacity, size, size), bf16),
            vmem((capacity, size, size), f32),
            vmem((capacity, size, slab_cols), bf16),
            vmem((slots, band, slab_cols), bf16),
            dma((6,)),
            dma((capacity,)),
            dma((peers, capacity, owners)),
            dma((peers, capacity, owners)),
            dma((peers, capacity, owners)),
            dma((peers, capacity, owners)),
            dma((peers, capacity, owners)),
            dma((peers, capacity, owners)),
            dma((capacity, owners)),
            dma((capacity, owners)),
        ],
        compiler_params=pltpu.CompilerParams(
            collective_id=0, has_side_effects=True, vmem_limit_bytes=60 * 1024 * 1024
        ),
    )(block_slot, grad, left_stat, right_stat, left_root, right_root, graft_acc)
    return pl.pallas_call(
        write_out,
        out_shape=tuple(jax.ShapeDtypeStruct(*r) for r in results),
        in_specs=[inside] * 4,
        out_specs=(anywhere,) * 4,
        scratch_shapes=[dma((4,))],
        compiler_params=pltpu.CompilerParams(vmem_limit_bytes=16 * 1024 * 1024),
    )(*held)


def solution(mesh):
    return jax.shard_map(
        local,
        mesh=mesh,
        in_specs=(
            P(None, "dp", None),
            P(),
            P("dp", "rep", None),
            P("dp", "rep", None),
            P("dp", None, None),
            P("dp", None, None),
            P("dp", None, None),
        ),
        out_specs=(
            P(None, "dp", "rep"),
            P("dp", "rep", None),
            P("dp", "rep", None),
            P("dp", None, None),
        ),
        check_vma=False,
    )
```

profile of v0, /device:TPU:0, one launch (start us, length us, event | category | flops | bytes accessed | tf_op | source)
XLA Modules:
  0.0 30.5 jit_solution(14386988327518226021)
XLA Ops:
  0.6 28.1 %shard_map.102 = (bf16[8,64,128]{2,1,0:T(8,128)(2,1)S(1)}, f32[2,128,512]{2,1,0:T(8,128)S(1)}, f32[2,128,512]{2,1,0:T(8,128)S(1)}, f32[2,512,512]{2,1,0:T(8,128)S(1)}) custom-call(s32[8]{0:T(128)} %slot_ref.1, bf16[8,64,512]{2,1,0:T(8,128)(2,1)} %grad_hbm.1, f32[2,128,512]{2,1,0:T(8,128)} %left_hbm.1, f32[2,128,512]{2,1,0:T(8,128)} %right_hbm.1, ...), custom_call_target="tpu_custom_call" | custom-call | tf_op jit(solution)/shard_map/pallas_call | solution.py:303
  28.7 1.7 %shard_map.103 = (bf16[8,64,128]{2,1,0:T(8,128)(2,1)}, f32[2,128,512]{2,1,0:T(8,128)}, f32[2,128,512]{2,1,0:T(8,128)}, f32[2,512,512]{2,1,0:T(8,128)}) custom-call(bf16[8,64,128]{2,1,0:T(8,128)(2,1)S(1)} %get-tuple-element.8.refs_0_, f32[2,128,512]{2,1,0:T(8,128)S(1)} %get-tuple-element.9.refs_1_, f32[2,128,512]{2,1,0:T(8,128)S(1)} %get-tuple-element.10.refs_2_, ...), custom_call_target="tpu_custom_call" | custom-call | tf_op jit(solution)/shard_map/pallas_call | solution.py:333
where the time goes:
time: 30.6 us; the launch traced here: 30.5 us
  Pallas kernels  29.8 us (97%)
  between operations  0.64 us (2%)
    pallas_call x1, Pallas kernels, local(): pl.pallas_call(functools.partial(kernel, owners, replicas), out_shape=tup...  28.1 us
    pallas_call x1, Pallas kernels, local(): pl.pallas_call(write_out, out_shape=tuple((jax.ShapeDtypeStruct(*r) for r...  1.74 us

commit v1 on v0

--- a/solution.py
+++ b/solution.py
@@ -67,7 +67,7 @@
     owners, replicas, slot_ref, grad_hbm, left_hbm, right_hbm, lroot_hbm, rroot_hbm, graft_hbm,
     update_ref, left, right, graft,
     own_grad, pack, placed, lroot, rroot, middle, precond, slab, returned,
-    load_sem, own_sem, send1, recv1, send_y, recv_y, send_c, recv_c, send3, recv3,
+    load_sem, send, recv1, recv_y, recv_c, recv3,
 ):
     me = lax.axis_index("dp")
     rep = lax.axis_index("rep")
@@ -133,23 +133,20 @@
     half = owners // 2
     far = sorted(range(half, owners), key=lambda k: (k % 2, k))
     near = list(range(1, half))
-    outward = []
-    firsts = {}
+    sent = [0] * 4
     for c in range(capacity):
         for k in far + near:
             to = flipped(me, k)
             for j in range(peers if k < half else 1):
                 copy = remote(
                     pack.at[j, to, c], placed.at[c, rows_of(me), cols_of(peer(j))],
-                    send1.at[j, c, k], recv1.at[j, c, k], (to, rep),
+                    send.at[0], recv1.at[c, k - 1], (to, rep),
                 )
                 copy.start()
-                firsts[j, c, k] = copy
-                outward.append(copy)
+                sent[0] += 1
 
     norms = [jnp.zeros((band // 4, size), jnp.float32) for _ in range(capacity)]
     squares = [jnp.zeros((1, 1), jnp.float32) for _ in range(capacity)]
-    thirds = {}
     tasks = []
 
     def multiply(c, q):
@@ -165,43 +162,39 @@
         mine = returned.at[me * capacity + c]
         for k in far + near:
             to = flipped(me, k)
-            thirds[c, k] = remote(slab.at[c, rows_of(to), :], mine, send3.at[c, k], recv3.at[c, k], (to, rep))
-            thirds[c, k].start()
-            outward.append(thirds[c, k])
-        thirds[c, 0] = pltpu.make_async_copy(slab.at[c, rows_of(me), :], mine, own_sem.at[c])
-        thirds[c, 0].start()
-
-    along_y = {}
-    across = {}
+            remote(slab.at[c, rows_of(to), :], mine, send.at[3], recv3.at[0], (to, rep)).start()
+            sent[3] += 1
+        returned[me * capacity + c] = slab[c, rows_of(me), :]
+
+    def bytes_of(pieces, sem):
+        rows = pieces * band * slab_cols // size
+        view = placed.at[0, pl.ds(0, rows), :]
+        return remote(view, view, sem, sem, (me, partner))
+
     def forward(c, k):
-        for j in range(peers if k < half else 1):
-            firsts[j, c, k].wait_recv()
+        bytes_of(peers if k < half else 1, recv1.at[c, k - 1]).wait_recv()
         rows = rows_of(flipped(me, k))
         if k >= half:
             piece = placed.at[c, rows, cols]
             for j in range(1, peers):
-                copy = remote(piece, piece, send_y.at[j, c, k], recv_y.at[j, c, k], (me, peer(j)))
-                copy.start()
-                along_y[j, c, k] = copy
+                remote(piece, piece, send.at[1], recv_y.at[j - 1, c, k - half], (me, peer(j))).start()
+                sent[1] += 1
         for j in range(peers if k < half else 1):
             piece = placed.at[c, rows, cols_of(peer(j))]
-            copy = remote(piece, piece, send_c.at[j, c, k], recv_c.at[j, c, k], (me, partner))
-            copy.start()
-            across[j, c, k] = copy
+            remote(piece, piece, send.at[2], recv_c.at[c, k - 1], (me, partner)).start()
+            sent[2] += 1
 
     def relay(c, k):
         for j in range(1, peers):
-            along_y[j, c, k].wait_recv()
+            bytes_of(1, recv_y.at[j - 1, c, k - half]).wait_recv()
             theirs = (rep + replicas - 2 * j) % replicas
             piece = placed.at[c, rows_of(flipped(me, k)), cols_of(theirs)]
-            copy = remote(piece, piece, send_c.at[j, c, k], recv_c.at[j, c, k], (me, partner))
-            copy.start()
-            across[j, c, k] = copy
+            remote(piece, piece, send.at[2], recv_c.at[c, k - 1], (me, partner)).start()
+            sent[2] += 1
 
     def absorb(c, k):
         if k > 0:
-            for j in range(peers):
-                across[j, c, k].wait_recv()
+            bytes_of(peers, recv_c.at[c, k - 1]).wait_recv()
         rows = rows_of(flipped(me, k))
         middle[c, rows, :] = jnp.dot(
             placed[c, rows, :], rroot[c], preferred_element_type=jnp.float32
@@ -255,17 +248,11 @@
         )
         right[c] = decay_rate * right[c] + (1.0 - decay_rate) * term
 
-    for copy in list(along_y.values()) + list(across.values()):
-        copy.wait_send()
-    for (c, k), copy in thirds.items():
-        if k == 0:
-            copy.wait()
-        else:
-            copy.wait_recv()
+    bytes_of(sent[3], recv3.at[0]).wait_recv()
     for b in range(blocks):
         update_ref[b] = returned[slot_ref[b]]
-    for copy in outward:
-        copy.wait_send()
+    for stage, pieces in enumerate(sent):
+        bytes_of(pieces, send.at[stage]).wait_send()
 
 
 def write_out(*refs):
@@ -316,15 +303,11 @@
             vmem((capacity, size, slab_cols), bf16),
             vmem((slots, band, slab_cols), bf16),
             dma((6,)),
-            dma((capacity,)),
-            dma((peers, capacity, owners)),
-            dma((peers, capacity, owners)),
-            dma((peers, capacity, owners)),
-            dma((peers, capacity, owners)),
-            dma((peers, capacity, owners)),
-            dma((peers, capacity, owners)),
-            dma((capacity, owners)),
-            dma((capacity, owners)),
+            dma((4,)),
+            dma((capacity, owners - 1)),
+            dma((peers - 1, capacity, owners // 2)),
+            dma((capacity, owners - 1)),
+            dma((1,)),
         ],
         compiler_params=pltpu.CompilerParams(
             collective_id=0, has_side_effects=True, vmem_limit_bytes=60 * 1024 * 1024

time: 30.6 us -> 28.9 us (0.944)
  Pallas kernels: 29.8 us -> 28.1 us
    pallas_call x1, Pallas kernels: 28.1 us -> 26.4 us  [local(): pl.pallas_call(functools.partial(kernel, owners, replicas), out_shape=tup...]
where the time goes in v1:
time: 28.9 us; the launch traced here: 28.8 us
  Pallas kernels  28.1 us (97%)
  between operations  0.64 us (2%)
    pallas_call x1, Pallas kernels, local(): pl.pallas_call(functools.partial(kernel, owners, replicas), out_shape=tup...  26.4 us
    pallas_call x1, Pallas kernels, local(): pl.pallas_call(write_out, out_shape=tuple((jax.ShapeDtypeStruct(*r) for r...  1.74 us

profile of v1, /device:TPU:0, one launch (start us, length us, event | category | flops | bytes accessed | tf_op | source)
XLA Modules:
  0.0 28.8 jit_solution(10158325346779907514)
XLA Ops:
  0.6 26.4 %shard_map.102 = (bf16[8,64,128]{2,1,0:T(8,128)(2,1)S(1)}, f32[2,128,512]{2,1,0:T(8,128)S(1)}, f32[2,128,512]{2,1,0:T(8,128)S(1)}, f32[2,512,512]{2,1,0:T(8,128)S(1)}) custom-call(s32[8]{0:T(128)} %slot_ref.1, bf16[8,64,512]{2,1,0:T(8,128)(2,1)} %grad_hbm.1, f32[2,128,512]{2,1,0:T(8,128)} %left_hbm.1, f32[2,128,512]{2,1,0:T(8,128)} %right_hbm.1, ...), custom_call_target="tpu_custom_call" | custom-call | tf_op jit(solution)/shard_map/pallas_call | solution.py:290
  27.0 1.7 %shard_map.103 = (bf16[8,64,128]{2,1,0:T(8,128)(2,1)}, f32[2,128,512]{2,1,0:T(8,128)}, f32[2,128,512]{2,1,0:T(8,128)}, f32[2,512,512]{2,1,0:T(8,128)}) custom-call(bf16[8,64,128]{2,1,0:T(8,128)(2,1)S(1)} %get-tuple-element.8.refs_0_, f32[2,128,512]{2,1,0:T(8,128)S(1)} %get-tuple-element.9.refs_1_, f32[2,128,512]{2,1,0:T(8,128)S(1)} %get-tuple-element.10.refs_2_, ...), custom_call_target="tpu_custom_call" | custom-call | tf_op jit(solution)/shard_map/pallas_call | solution.py:316

commit v2 on v1

--- a/solution.py
+++ b/solution.py
@@ -64,10 +64,10 @@
 
 
 def kernel(
-    owners, replicas, slot_ref, grad_hbm, left_hbm, right_hbm, lroot_hbm, rroot_hbm, graft_hbm,
+    owners, replicas, slot_hbm, grad_hbm, left_hbm, right_hbm, lroot_hbm, rroot_hbm, graft_hbm,
     update_ref, left, right, graft,
-    own_grad, pack, placed, lroot, rroot, middle, precond, slab, returned,
-    load_sem, send, recv1, recv_y, recv_c, recv3,
+    slot_ref, own_grad, pack, placed, lroot, rroot, norm_parts, precond, slab, returned,
+    load_sem, send, recv1, recv_y, recv_c, recv_n, recv3,
 ):
     me = lax.axis_index("dp")
     rep = lax.axis_index("rep")
@@ -92,15 +92,18 @@
             device_id=device, device_id_type=pl.DeviceIdType.MESH,
         )
 
+    grad_load = pltpu.make_async_copy(grad_hbm, own_grad, load_sem.at[0])
+    grad_load.start()
+    slot_load = pltpu.make_async_copy(slot_hbm, slot_ref, load_sem.at[6])
+    slot_load.start()
     cols = cols_of(rep)
     barrier = pltpu.get_barrier_semaphore()
     others = [(flipped(me, k), rep) for k in range(1, owners)]
-    others += [(me, partner)] + [(me, peer(j)) for j in range(1, peers)]
+    group = [(me, (rep + j) % replicas) for j in range(1, replicas)]
+    others += group
     for device in others:
         pl.semaphore_signal(barrier, inc=1, device_id=device, device_id_type=pl.DeviceIdType.MESH)
 
-    grad_load = pltpu.make_async_copy(grad_hbm, own_grad, load_sem.at[0])
-    grad_load.start()
     loads = []
     for n, (src, dst) in enumerate(
         ((graft_hbm, graft), (rroot_hbm, rroot), (lroot_hbm, lroot), (left_hbm, left), (right_hbm, right))
@@ -108,6 +111,7 @@
         loads.append(pltpu.make_async_copy(src, dst, load_sem.at[n + 1]))
         loads[n].start()
 
+    slot_load.wait()
     grad_load.wait()
     def find(slot):
         block = jnp.int32(0)
@@ -133,7 +137,7 @@
     half = owners // 2
     far = sorted(range(half, owners), key=lambda k: (k % 2, k))
     near = list(range(1, half))
-    sent = [0] * 4
+    sent = [0] * 5
     for c in range(capacity):
         for k in far + near:
             to = flipped(me, k)
@@ -144,27 +148,6 @@
                 )
                 copy.start()
                 sent[0] += 1
-
-    norms = [jnp.zeros((band // 4, size), jnp.float32) for _ in range(capacity)]
-    squares = [jnp.zeros((1, 1), jnp.float32) for _ in range(capacity)]
-    tasks = []
-
-    def multiply(c, q):
-        part = pl.ds(q * size, size)
-        full = jnp.dot(lroot[c, part, :], middle[c], preferred_element_type=jnp.float32)
-        precond[c, part, :] = full
-        squares[c] = squares[c] + jnp.sum(full * full, axis=(0, 1), keepdims=True)
-
-    def finish(c):
-        graft_norm = jnp.sqrt(jnp.sum(norms[c], axis=(0, 1), keepdims=True))
-        scale = graft_norm / (jnp.sqrt(squares[c]) + epsilon)
-        slab[c] = (scale * precond[c, :, cols]).astype(jnp.bfloat16)
-        mine = returned.at[me * capacity + c]
-        for k in far + near:
-            to = flipped(me, k)
-            remote(slab.at[c, rows_of(to), :], mine, send.at[3], recv3.at[0], (to, rep)).start()
-            sent[3] += 1
-        returned[me * capacity + c] = slab[c, rows_of(me), :]
 
     def bytes_of(pieces, sem):
         rows = pieces * band * slab_cols // size
@@ -181,7 +164,7 @@
                 sent[1] += 1
         for j in range(peers if k < half else 1):
             piece = placed.at[c, rows, cols_of(peer(j))]
-            remote(piece, piece, send.at[2], recv_c.at[c, k - 1], (me, partner)).start()
+            remote(piece, piece, send.at[2], recv_c.at[c, k // half], (me, partner)).start()
             sent[2] += 1
 
     def relay(c, k):
@@ -189,55 +172,82 @@
             bytes_of(1, recv_y.at[j - 1, c, k - half]).wait_recv()
             theirs = (rep + replicas - 2 * j) % replicas
             piece = placed.at[c, rows_of(flipped(me, k)), cols_of(theirs)]
-            remote(piece, piece, send.at[2], recv_c.at[c, k - 1], (me, partner)).start()
+            remote(piece, piece, send.at[2], recv_c.at[c, k // half], (me, partner)).start()
             sent[2] += 1
 
-    def absorb(c, k):
-        if k > 0:
-            bytes_of(peers, recv_c.at[c, k - 1]).wait_recv()
+    norms = [jnp.zeros((8, slab_cols), jnp.float32) for _ in range(capacity)]
+
+    def measure(c, k):
         rows = rows_of(flipped(me, k))
-        middle[c, rows, :] = jnp.dot(
+        wide = placed[c, rows, cols].astype(jnp.float32)
+        fresh = decay_rate * graft[c, rows, cols] + (1.0 - decay_rate) * wide * wide
+        direction = wide / (jnp.sqrt(fresh) + epsilon)
+        norms[c] = norms[c] + jnp.sum((direction * direction).reshape(band // 8, 8, slab_cols), axis=0)
+
+    def share(c):
+        norm_parts[c * replicas + rep] = norms[c]
+        mine = norm_parts.at[c * replicas + rep]
+        for device in group:
+            remote(mine, mine, send.at[4], recv_n.at[c], device).start()
+            sent[4] += 1
+
+    def tiles_of(count, sem):
+        view = norm_parts.at[pl.ds(0, count)]
+        return remote(view, view, sem, sem, (me, partner))
+
+    def half_rows(side):
+        start = (me // half + side) % 2
+        return pl.ds(pl.multiple_of(start * half * band, half * band), half * band)
+
+    def product(c, side):
+        rows = half_rows(side)
+        middle = jnp.dot(
             placed[c, rows, :], rroot[c], preferred_element_type=jnp.float32
         ).astype(jnp.bfloat16)
-        for g in range(4):
-            part = pl.ds(pl.multiple_of(flipped(me, k) * band + g * (band // 4), band // 4), band // 4)
-            wide = placed[c, part, :].astype(jnp.float32)
-            fresh = decay_rate * graft[c, part, :] + (1.0 - decay_rate) * wide * wide
-            graft[c, part, :] = fresh
-            direction = wide / (jnp.sqrt(fresh) + epsilon)
-            norms[c] = norms[c] + direction * direction
-        left_over[c] -= 1
-        if left_over[c] == 0:
-            tasks.extend(functools.partial(multiply, c, q) for q in range(1))
-            tasks.append(functools.partial(finish, c))
-
-    left_over = [owners] * capacity
-    arrivals = near[:1] + far[:1] + near[1:2] + far[1:2] + near[2:] + far[2:]
-    lag_y = 8
-    lag_c = 5
-    events = []
-    for n, (c, k) in enumerate((c, k) for c in range(capacity) for k in arrivals):
-        events.append((n, 0, forward, c, k))
-        if k >= half:
-            events.append((n + lag_y, 1, relay, c, k))
-        events.append((n + lag_c + (lag_y if k >= half else 0), 2, absorb, c, k))
-    events.sort(key=lambda event: event[:2])
-    begun = 0
-    for event in events:
-        if event[2] is absorb and not begun:
-            begun = 1
-            for load in loads[:3]:
-                load.wait()
-            for c in range(capacity):
-                absorb(c, 0)
-        if tasks:
-            tasks.pop(0)()
-        event[2](*event[3:])
-    for task in tasks:
-        task()
+        return jnp.dot(lroot[c, :, rows], middle, preferred_element_type=jnp.float32)
+
+    def begin(c):
+        bytes_of(peers * (half - 1), recv_c.at[c, 0]).wait_recv()
+        precond[c] = product(c, 0)
+
+    def complete(c):
+        bytes_of(peers * half, recv_c.at[c, 1]).wait_recv()
+        full = precond[c] + product(c, 1)
+        precond[c] = full
+        squares = jnp.sum(full * full, axis=(0, 1), keepdims=True)
+        tiles_of(replicas - 1, recv_n.at[c]).wait_recv()
+        total = jnp.sum(norm_parts[pl.ds(c * replicas, replicas)], axis=0)
+        graft_norm = jnp.sqrt(jnp.sum(total, axis=(0, 1), keepdims=True))
+        scale = graft_norm / (jnp.sqrt(squares) + epsilon)
+        slab[c] = (scale * precond[c, :, cols]).astype(jnp.bfloat16)
+        mine = returned.at[me * capacity + c]
+        for k in far + near:
+            to = flipped(me, k)
+            remote(slab.at[c, rows_of(to), :], mine, send.at[3], recv3.at[0], (to, rep)).start()
+            sent[3] += 1
+        returned[me * capacity + c] = slab[c, rows_of(me), :]
+
+    for load in loads[:3]:
+        load.wait()
+    for c in range(capacity):
+        measure(c, 0)
+    plan = [('f', 0, 1), ('f', 0, 4), ('f', 0, 2), ('f', 0, 6), ('f', 0, 5), ('f', 0, 7), ('f', 0, 3), ('n', 0, 0), ('f', 1, 4), ('f', 1, 1), ('r', 0, 4), ('f', 1, 6), ('f', 1, 2), ('r', 0, 6), ('f', 1, 5), ('f', 1, 7), ('f', 1, 3), ('n', 1, 0), ('b', 0, 0), ('r', 0, 5), ('r', 0, 7), ('r', 1, 4), ('r', 1, 6), ('c', 0, 0), ('r', 1, 5), ('r', 1, 7), ('b', 1, 0), ('c', 1, 0)]
+    for name, c, k in plan:
+        if name == "f":
+            forward(c, k)
+            measure(c, k)
+        elif name == "r":
+            relay(c, k)
+        else:
+            {"n": share, "b": begin, "c": complete}[name](c)
 
     loads[3].wait()
     loads[4].wait()
+    for c in range(capacity):
+        for g in range(owners):
+            part = pl.ds(g * band, band)
+            wide = placed[c, part, :].astype(jnp.float32)
+            graft[c, part, :] = decay_rate * graft[c, part, :] + (1.0 - decay_rate) * wide * wide
     for c in range(capacity):
         term = lax.dot_general(
             placed[c, cols, :], placed[c], (((1,), (1,)), ((), ())), preferred_element_type=jnp.float32
@@ -251,8 +261,9 @@
     bytes_of(sent[3], recv3.at[0]).wait_recv()
     for b in range(blocks):
         update_ref[b] = returned[slot_ref[b]]
-    for stage, pieces in enumerate(sent):
+    for stage, pieces in enumerate(sent[:4]):
         bytes_of(pieces, send.at[stage]).wait_send()
+    tiles_of(sent[4], send.at[4]).wait_send()
 
 
 def write_out(*refs):
@@ -290,23 +301,25 @@
     held = pl.pallas_call(
         functools.partial(kernel, owners, replicas),
         out_shape=tuple(vmem(*r) for r in results),
-        in_specs=[pl.BlockSpec(memory_space=pltpu.SMEM)] + [anywhere] * 6,
+        in_specs=[anywhere] * 7,
         out_specs=(inside,) * 4,
         scratch_shapes=[
+            pltpu.SMEM(block_slot.shape, jnp.int32),
             vmem((blocks, band, size), bf16),
             vmem((peers, owners, capacity, band, slab_cols), bf16),
             vmem((capacity, size, size), bf16),
             vmem(left_root.shape, bf16),
             vmem(right_root.shape, bf16),
-            vmem((capacity, size, size), bf16),
+            vmem((capacity * replicas, 8, slab_cols), f32),
             vmem((capacity, size, size), f32),
             vmem((capacity, size, slab_cols), bf16),
             vmem((slots, band, slab_cols), bf16),
-            dma((6,)),
-            dma((4,)),
+            dma((7,)),
+            dma((5,)),
             dma((capacity, owners - 1)),
             dma((peers - 1, capacity, owners // 2)),
-            dma((capacity, owners - 1)),
+            dma((capacity, 2)),
+            dma((capacity,)),
             dma((1,)),
         ],
         compiler_params=pltpu.CompilerParams(

time: 28.9 us -> 27.9 us (0.965)
  Pallas kernels: 28.1 us -> 27.2 us
    pallas_call x1, Pallas kernels: 26.4 us -> 25.4 us  [local(): pl.pallas_call(functools.partial(kernel, owners, replicas), out_shape=tup...]
where the time goes in v2:
time: 27.9 us; the launch traced here: 27.8 us
  Pallas kernels  27.2 us (97%)
  between operations  0.64 us (2%)
    pallas_call x1, Pallas kernels, local(): pl.pallas_call(functools.partial(kernel, owners, replicas), out_shape=tup...  25.4 us
    pallas_call x1, Pallas kernels, local(): pl.pallas_call(write_out, out_shape=tuple((jax.ShapeDtypeStruct(*r) for r...  1.74 us

profile of v2, /device:TPU:0, one launch (start us, length us, event | category | flops | bytes accessed | tf_op | source)
XLA Modules:
  0.0 27.8 jit_solution(2108628491406406753)
XLA Ops:
  0.6 25.4 %shard_map.102 = (bf16[8,64,128]{2,1,0:T(8,128)(2,1)S(1)}, f32[2,128,512]{2,1,0:T(8,128)S(1)}, f32[2,128,512]{2,1,0:T(8,128)S(1)}, f32[2,512,512]{2,1,0:T(8,128)S(1)}) custom-call(s32[8]{0:T(128)} %slot_hbm.1, bf16[8,64,512]{2,1,0:T(8,128)(2,1)} %grad_hbm.1, f32[2,128,512]{2,1,0:T(8,128)} %left_hbm.1, f32[2,128,512]{2,1,0:T(8,128)} %right_hbm.1, ...), custom_call_target="tpu_custom_call" | custom-call | tf_op jit(solution)/shard_map/pallas_call | solution.py:301
  26.1 1.7 %shard_map.103 = (bf16[8,64,128]{2,1,0:T(8,128)(2,1)}, f32[2,128,512]{2,1,0:T(8,128)}, f32[2,128,512]{2,1,0:T(8,128)}, f32[2,512,512]{2,1,0:T(8,128)}) custom-call(bf16[8,64,128]{2,1,0:T(8,128)(2,1)S(1)} %get-tuple-element.8.refs_0_, f32[2,128,512]{2,1,0:T(8,128)S(1)} %get-tuple-element.9.refs_1_, f32[2,128,512]{2,1,0:T(8,128)S(1)} %get-tuple-element.10.refs_2_, ...), custom_call_target="tpu_custom_call" | custom-call | tf_op jit(solution)/shard_map/pallas_call | solution.py:329

commit v3 on v2

--- a/solution.py
+++ b/solution.py
@@ -98,7 +98,7 @@
     slot_load.start()
     cols = cols_of(rep)
     barrier = pltpu.get_barrier_semaphore()
-    others = [(flipped(me, k), rep) for k in range(1, owners)]
+    others = [(flipped(me, k), rep) for k in reversed(range(1, owners))]
     group = [(me, (rep + j) % replicas) for j in range(1, replicas)]
     others += group
     for device in others:
@@ -135,7 +135,7 @@
     pl.semaphore_wait(barrier, len(others))
 
     half = owners // 2
-    far = sorted(range(half, owners), key=lambda k: (k % 2, k))
+    far = list(reversed(range(half, owners)))
     near = list(range(1, half))
     sent = [0] * 5
     for c in range(capacity):
@@ -212,9 +212,18 @@
 
     def complete(c):
         bytes_of(peers * half, recv_c.at[c, 1]).wait_recv()
-        full = precond[c] + product(c, 1)
-        precond[c] = full
-        squares = jnp.sum(full * full, axis=(0, 1), keepdims=True)
+        rows = half_rows(1)
+        middle = jnp.dot(
+            placed[c, rows, :], rroot[c], preferred_element_type=jnp.float32
+        ).astype(jnp.bfloat16)
+        folded = jnp.zeros((8, size), jnp.float32)
+        step = size // 4
+        for q in range(4):
+            part = pl.ds(q * step, step)
+            full = precond[c, part, :] + jnp.dot(lroot[c, part, rows], middle, preferred_element_type=jnp.float32)
+            precond[c, part, :] = full
+            folded = folded + jnp.sum((full * full).reshape(step // 8, 8, size), axis=0)
+        squares = jnp.sum(folded, axis=(0, 1), keepdims=True)
         tiles_of(replicas - 1, recv_n.at[c]).wait_recv()
         total = jnp.sum(norm_parts[pl.ds(c * replicas, replicas)], axis=0)
         graft_norm = jnp.sqrt(jnp.sum(total, axis=(0, 1), keepdims=True))
@@ -231,7 +240,18 @@
         load.wait()
     for c in range(capacity):
         measure(c, 0)
-    plan = [('f', 0, 1), ('f', 0, 4), ('f', 0, 2), ('f', 0, 6), ('f', 0, 5), ('f', 0, 7), ('f', 0, 3), ('n', 0, 0), ('f', 1, 4), ('f', 1, 1), ('r', 0, 4), ('f', 1, 6), ('f', 1, 2), ('r', 0, 6), ('f', 1, 5), ('f', 1, 7), ('f', 1, 3), ('n', 1, 0), ('b', 0, 0), ('r', 0, 5), ('r', 0, 7), ('r', 1, 4), ('r', 1, 6), ('c', 0, 0), ('r', 1, 5), ('r', 1, 7), ('b', 1, 0), ('c', 1, 0)]
+    ahead = far[: half // 2]
+    order = near[:1] + ahead + near[1:2] + far[half // 2 :] + near[2:]
+    plan = [("f", 0, k) for k in order] + [("n", 0, 0)]
+    for c in range(1, capacity):
+        for n, k in enumerate(far):
+            plan.append(("f", c, k))
+            if n % 2:
+                plan.append(("r", c - 1, far[n // 2]))
+        plan += [("f", c, k) for k in near] + [("n", c, 0), ("b", c - 1, 0)]
+        plan += [("r", c - 1, k) for k in far[half // 2 :]] + [("c", c - 1, 0)]
+    plan += [("r", capacity - 1, k) for k in far]
+    plan += [("b", capacity - 1, 0), ("c", capacity - 1, 0)]
     for name, c, k in plan:
         if name == "f":
             forward(c, k)
@@ -283,7 +303,8 @@
     capacity = left_stat.shape[0]
     slab_cols = size // replicas
     power_of_two = owners & (owners - 1) == 0 and owners >= 4
-    if slab_cols % 128 or band % 64 or replicas % 2 or not power_of_two:
+    fits = capacity * (owners - 1) * band <= 2 * size
+    if slab_cols % 128 or band % 64 or replicas % 2 or not power_of_two or not fits:
         return local_plain(grad, block_slot, left_stat, right_stat, left_root, right_root, graft_acc)
     peers = replicas // 2
     slots = owners * capacity

time: 27.9 us -> 27.1 us (0.971)
  Pallas kernels: 27.2 us -> 26.3 us
    pallas_call x1, Pallas kernels: 25.4 us -> 24.5 us  [local(): pl.pallas_call(functools.partial(kernel, owners, replicas), out_shape=tup...]
where the time goes in v3:
time: 27.1 us; the launch traced here: 26.9 us
  Pallas kernels  26.3 us (97%)
  between operations  0.64 us (2%)
    pallas_call x1, Pallas kernels, local(): pl.pallas_call(functools.partial(kernel, owners, replicas), out_shape=tup...  24.5 us
    pallas_call x1, Pallas kernels, local(): pl.pallas_call(write_out, out_shape=tuple((jax.ShapeDtypeStruct(*r) for r...  1.74 us

profile of v3, /device:TPU:0, one launch (start us, length us, event | category | flops | bytes accessed | tf_op | source)
XLA Modules:
  0.0 26.9 jit_solution(16986562650389789302)
XLA Ops:
  0.6 24.5 %shard_map.102 = (bf16[8,64,128]{2,1,0:T(8,128)(2,1)S(1)}, f32[2,128,512]{2,1,0:T(8,128)S(1)}, f32[2,128,512]{2,1,0:T(8,128)S(1)}, f32[2,512,512]{2,1,0:T(8,128)S(1)}) custom-call(s32[8]{0:T(128)} %slot_hbm.1, bf16[8,64,512]{2,1,0:T(8,128)(2,1)} %grad_hbm.1, f32[2,128,512]{2,1,0:T(8,128)} %left_hbm.1, f32[2,128,512]{2,1,0:T(8,128)} %right_hbm.1, ...), custom_call_target="tpu_custom_call" | custom-call | tf_op jit(solution)/shard_map/pallas_call | solution.py:322
  25.2 1.7 %shard_map.103 = (bf16[8,64,128]{2,1,0:T(8,128)(2,1)}, f32[2,128,512]{2,1,0:T(8,128)}, f32[2,128,512]{2,1,0:T(8,128)}, f32[2,512,512]{2,1,0:T(8,128)}) custom-call(bf16[8,64,128]{2,1,0:T(8,128)(2,1)S(1)} %get-tuple-element.8.refs_0_, f32[2,128,512]{2,1,0:T(8,128)S(1)} %get-tuple-element.9.refs_1_, f32[2,128,512]{2,1,0:T(8,128)S(1)} %get-tuple-element.10.refs_2_, ...), custom_call_target="tpu_custom_call" | custom-call | tf_op jit(solution)/shard_map/pallas_call | solution.py:350
